TPU v7x, 256 devices: a whole 4x4x8 slice. The times are simulated.
256 devices in a mesh: seq: 32 (over x, y, core), head: 8 (over z).
Axes of the slice: x: 4, y: 4, z: 8, core: 2. Of those that a mesh axis runs over, the one named last changes fastest.
Arguments:
- queries: bfloat16 [24576, 8192], P('seq', 'head'), may hold values from -140 to 140
- key_weight: bfloat16 [1024, 8192], P(None, 'head'), may hold values from -0.1875 to 0.1875
- value_weight: bfloat16 [1024, 8192], P(None, 'head'), may hold values from -0.1875 to 0.1875
- encodings: bfloat16 [256, 128, 1024], P('seq', None, 'head'), may hold values from -6 to 6
- nb_owner: int32 [384, 2], P('seq'), may hold values from 0 to 31, all different within a row; in each aligned block of 12 rows (0 to 11, 12 to 23, ...) at most 2 rows name the same one
- nb_block: int32 [384, 2], P('seq'), may hold values from 0 to 7
Outputs:
- attended: bfloat16 [24576, 8192], P('seq', 'head')
Inputs may be any that keep to these rules, and one draw needn't show every extreme that they name: `nb_owner`: the 2 neighbours of a span have different owners. Among the spans of one device no owner is named more than 2 times, and in every draw some device names some owner exactly 2 times.
All inputs are finite; a program needn't handle non-finite values.
Results may differ from a plain program's by a relative error of at most 0.012.
The roundings to bfloat16 on the way count: a program that leaves them out, or rounds other values in their place, can miss the bound.
Values may be sent and summed in bfloat16 or wider, within the bound.
A program may use at most 128 MiB of HBM per device.

v0:
```python
import math
import jax
import jax.numpy as jnp
from jax import lax
from jax.sharding import PartitionSpec as P

HEAD_DIM = 128
SPAN = 64


def shifted(shard, axis, by):
    devices = lax.axis_size(axis)
    pairs = [(i, i + by) for i in range(devices) if 0 <= i + by < devices]
    return lax.ppermute(shard, axis, pairs)


def on_device(queries, key_weight, value_weight, encodings, nb_owner, nb_block):
    span_dev, neighbours = nb_owner.shape
    entries = span_dev * neighbours
    db_local, block_len, slice_width = encodings.shape
    group_width = key_weight.shape[1]
    group_heads = group_width // HEAD_DIM
    peer_count = lax.axis_size("seq")
    slot_most = max(2, (entries + peer_count - 1) // peer_count)
    owner_ids = nb_owner.reshape(entries)
    block_ids = nb_block.reshape(entries)
    position = jnp.arange(entries, dtype=jnp.int32)
    same_owner = owner_ids[:, None] == owner_ids[None, :]
    before = position[None, :] < position[:, None]
    slot_ids = jnp.sum((same_owner & before).astype(jnp.int32), axis=1)
    owner_hit = owner_ids[:, None] == jnp.arange(peer_count, dtype=jnp.int32)[None, :]
    slot_hit = slot_ids[:, None] == jnp.arange(slot_most, dtype=jnp.int32)[None, :]
    marked = owner_hit[:, :, None] & slot_hit[:, None, :]
    requests = jnp.sum(jnp.where(marked, (block_ids + 1)[:, None, None], 0), axis=0)
    asked_ids = lax.all_to_all(requests, "seq", split_axis=0, concat_axis=0, tiled=True)
    present = asked_ids > 0
    picked = jnp.take(encodings, jnp.maximum(asked_ids - 1, 0), axis=0)
    picked = jnp.where(present[:, :, None, None], picked, jnp.zeros_like(picked))
    replies = lax.all_to_all(picked, "seq", split_axis=0, concat_axis=0, tiled=True)
    slot_count = replies.shape[1]
    flat_rows = replies.reshape(peer_count * slot_count, block_len, slice_width)
    compact = jnp.take(flat_rows, owner_ids * slot_count + slot_ids, axis=0)
    full_width = lax.all_gather(compact, "head", axis=2, tiled=True)
    rows = full_width.reshape(-1, full_width.shape[2])
    key_rows = jnp.dot(rows, key_weight, preferred_element_type=jnp.float32).astype(jnp.bfloat16)
    value_rows = jnp.dot(rows, value_weight, preferred_element_type=jnp.float32).astype(
        jnp.bfloat16
    )
    key_rows, value_rows = (
        key_rows.reshape(span_dev, neighbours * block_len, group_heads, HEAD_DIM),
        value_rows.reshape(span_dev, neighbours * block_len, group_heads, HEAD_DIM),
    )
    stacked = jnp.stack([key_rows[span_dev - 1], value_rows[span_dev - 1]])
    earlier = shifted(stacked, "seq", 1)
    key_rows = jnp.concatenate([earlier[0][None], key_rows], axis=0)
    value_rows = jnp.concatenate([earlier[1][None], value_rows], axis=0)
    token_count = queries.shape[0]
    grouped = jnp.pad(queries, ((1, SPAN - 1), (0, 0))).reshape(
        span_dev + 1, SPAN, group_heads, HEAD_DIM
    )
    scores = jnp.einsum(
        "cqhd,ckhd->chqk", grouped, key_rows, preferred_element_type=jnp.float32
    ) * (1.0 / math.sqrt(HEAD_DIM))
    weights = jax.nn.softmax(scores, axis=-1).astype(jnp.bfloat16)
    attended = jnp.einsum(
        "chqk,ckhd->cqhd", weights, value_rows, preferred_element_type=jnp.float32
    )
    attended = attended.reshape((span_dev + 1) * SPAN, group_width)[1 : token_count + 1]
    return attended.astype(jnp.bfloat16)


def solution(mesh):
    return jax.shard_map(
        on_device,
        mesh=mesh,
        in_specs=(
            P("seq", "head"),
            P(None, "head"),
            P(None, "head"),
            P("seq", None, "head"),
            P("seq", None),
            P("seq", None),
        ),
        out_specs=P("seq", "head"),
        check_vma=False,
    )
```

profile of v0, /device:TPU:1, one launch (start us, length us, event | category | flops | bytes accessed | tf_op | source)
XLA Modules:
  0.0 267.6 jit_solution(14205049635166241465)
XLA Ops:
  8.9 15.3 %all_to_all.14 = s32[32,1,2]{2,1,0:T(1,128)S(1)} all-to-all(s32[32,1,2]{2,1,0:T(1,128)S(1)} %copy.65), channel_id=1, replica_groups=mesh['seq'=32,'head'=8] {'seq'}, dimensions={0} | all-to-all | bytes 512 | tf_op jit(solution)/shard_map/all_to_all | solution.py:35
  24.7 3.1 %gather_fusion = bf16[64,128,128]{2,1,0:T(8,128)(2,1)} fusion(bf16[8,128,128]{2,1,0:T(8,128)(2,1)} %param.9, s32[1024]{0:T(1024)S(1)} %pad_clamp_fusion.1), kind=kCustom, calls=%fused_computation | custom fusion | bytes 4194560 | tf_op jit(solution)/shard_map/jit(_take)/gather | solution.py:37
  27.8 3.3 %select_select_fusion = bf16[32,2,128,128]{3,2,1,0:T(8,128)(2,1)} fusion(bf16[32,2,128,128]{3,2,1,0:T(8,128)(2,1)} %bitcast.37, pred[32,2]{1,0:T(8,128)(4,1)S(1)} %copy.69, pred[32,2]{1,0:T(8,128)(4,1)S(1)} %copy.67), kind=kLoop, calls=%fused_computation.19 | loop fusion | flops 2097152 | bytes 4194432 | tf_op jit(solution)/shard_map/jit(_where)/select_n | solution.py:38
  31.1 5.0 %all-to-all-start.1 = ((bf16[32,2,128,128]{3,2,1,0:T(8,128)(2,1)}), bf16[32,2,128,128]{3,2,1,0:T(8,128)(2,1)}, u32[]{:S(2)}, u32[]{:S(2)}) async-start(bf16[32,2,128,128]{3,2,1,0:T(8,128)(2,1)} %select_select_fusion), calls=%async_computation.1 | async-start | bytes 4194304 | tf_op jit(solution)/shard_map/all_to_all | solution.py:39
  36.4 28.2 %all-to-all-done.1 = bf16[32,2,128,128]{3,2,1,0:T(8,128)(2,1)} async-done(((bf16[32,2,128,128]{3,2,1,0:T(8,128)(2,1)}), bf16[32,2,128,128]{3,2,1,0:T(8,128)(2,1)}, u32[]{:S(2)}, u32[]{:S(2)}) %all-to-all-start.1) | async-done | bytes 2097184 | tf_op jit(solution)/shard_map/all_to_all | solution.py:39
  64.5 2.3 gather_fusion.1
  67.9 75.7 %all-gather.2.cloned.1.call-done = bf16[24,128,1024]{2,1,0:T(8,128)(2,1)} async-done(((bf16[24,128,128]{2,1,0:T(8,128)(2,1)}), bf16[24,128,1024]{2,1,0:T(8,128)(2,1)}) %all-gather.2.cloned.1.call-update) | async-done | bytes 6291472 | tf_op jit(solution)/shard_map/all_gather | solution.py:43
  143.6 9.8 %convolution_convert_fusion.1 = bf16[3072,1024]{0,1:T(8,128)(2,1)S(1)} fusion(bf16[3072,1024]{1,0:T(8,128)(2,1)} %bitcast.44, bf16[1024,1024]{1,0:T(8,128)(2,1)S(1)} %copy-done), kind=kOutput, calls=%fused_computation.16 | convolution fusion | flops 6445596672 | bytes 14680064 | tf_op jit(solution)/shard_map/dot_general | solution.py:45
  153.4 2.6 copy-done.2
  156.4 9.5 %convolution_convert_fusion = bf16[3072,1024]{0,1:T(8,128)(2,1)S(1)} fusion(bf16[3072,1024]{1,0:T(8,128)(2,1)} %bitcast.45, bf16[1024,1024]{1,0:T(8,128)(2,1)} %param.8), kind=kOutput, calls=%fused_computation.15 | convolution fusion | flops 6445596672 | bytes 14680064 | tf_op jit(solution)/shard_map/dot_general | solution.py:46
  165.9 2.6 copy-done.3
  170.0 6.6 %collective-permute-start = (bf16[2,256,8,128]{3,1,2,0:T(8,128)(2,1)}, bf16[2,256,8,128]{3,1,2,0:T(8,128)(2,1)S(1)}, u32[]{:S(2)}, u32[]{:S(2)}) collective-permute-start(bf16[2,256,8,128]{3,1,2,0:T(8,128)(2,1)} %pad_maximum_fusion), channel_id=1, source_target_pairs={{0,8},{8,16},{16,24},{24,32},{32,40},{40,48},{48,56},{56,64},{64,7... | collective-permute-start | bytes 3145736 | tf_op jit(solution)/shard_map/ppermute | solution.py:14
  176.6 1.9 pad_bitcast_fusion
  178.5 1.7 copy.84
  180.2 12.0 %reshape.175 = bf16[12,256,8,128]{1,0,3,2:T(8,128)(2,1)} reshape(bf16[3072,1024]{0,1:T(8,128)(2,1)} %copy-done.2) | data formatting | bytes 12582912 | tf_op jit(solution)/shard_map/reshape | solution.py:50
  192.2 12.0 %reshape.174 = bf16[12,256,8,128]{1,0,3,2:T(8,128)(2,1)} reshape(bf16[3072,1024]{0,1:T(8,128)(2,1)} %copy-done.3) | data formatting | bytes 12582912 | tf_op jit(solution)/shard_map/reshape | solution.py:51
  204.3 11.9 %copy.77 = bf16[12,256,8,128]{3,1,2,0:T(8,128)(2,1)} copy(bf16[12,256,8,128]{1,0,3,2:T(8,128)(2,1)} %reshape.175) | data formatting | bytes 12582912 | tf_op jit(solution)/shard_map/reshape | solution.py:50
  216.2 12.1 %copy.75 = bf16[12,256,8,128]{3,1,2,0:T(8,128)(2,1)} copy(bf16[12,256,8,128]{1,0,3,2:T(8,128)(2,1)} %reshape.174) | data formatting | bytes 12582912 | tf_op jit(solution)/shard_map/reshape | solution.py:51
  229.1 4.5 %fusion.1 = f32[13,8,64,256]{3,2,1,0:T(8,128)S(1)} fusion(bf16[12,256,8,128]{3,1,2,0:T(8,128)(2,1)} %copy.77, bf16[1,256,8,128]{3,1,2,0:T(8,128)(2,1)S(1)} %get-tuple-element.5, bf16[13,64,8,128]{3,2,1,0:T(8,128)(2,1)S(1)} %bitcast.39), kind=kOutput, calls=%fused_computation.3 | convolution fusion | flops 439615488 | bytes 15335424 | tf_op jit(solution)/shard_map/cqhd,ckhd->chqk/dot_general | solution.py:61
  233.7 2.8 %copy-done.4 = f32[13,8,64,256]{3,2,1,0:T(8,128)} copy-done((f32[13,8,64,256]{3,2,1,0:T(8,128)}, f32[13,8,64,256]{3,2,1,0:T(8,128)S(1)}, u32[]{:S(2)}) %copy-start.4) | copy-done | bytes 6815768
  236.4 2.6 fusion.34
  239.0 16.8 %fusion.18 = bf16[13,64,8,128]{3,1,2,0:T(8,128)(2,1)} fusion(bf16[12,256,8,128]{3,1,2,0:T(8,128)(2,1)} %copy.75, bf16[1,256,8,128]{3,1,2,0:T(8,128)(2,1)S(1)} %copy-done.6, f32[13,8,64]{2,1,0:T(8,128)S(1)} %fusion.34, f32[13,8,64,256]{3,2,1,0:T(8,128)} %copy-done.4), kind=kOutput, calls=%fused_computation.24 | convolution fusion | flops 459217664 | bytes 15362048 | tf_op jit(solution)/shard_map/chqk,ckhd->cqhd/dot_general | solution.py:65
  255.8 2.8 %copy.79 = bf16[13,64,8,128]{3,2,1,0:T(8,128)(2,1)S(1)} copy(bf16[13,64,8,128]{3,1,2,0:T(8,128)(2,1)} %fusion.18) | data formatting | bytes 3407872 | tf_op jit(solution)/shard_map/chqk,ckhd->cqhd/transpose | solution.py:65
  259.1 1.6 slice.37
  (48 shorter events, 7.2 us)
Async XLA Ops:
  6.5 137.0 %copy-start = (bf16[1024,1024]{1,0:T(8,128)(2,1)S(1)}, bf16[1024,1024]{1,0:T(8,128)(2,1)}, u32[]{:S(2)}) copy-start(bf16[1024,1024]{1,0:T(8,128)(2,1)} %param.7) | copy-start | bytes 6291460
  24.7 11.4 %copy-start.7 = (s32[12,2]{0,1:T(2,128)S(1)}, s32[12,2]{0,1:T(2,128)}, u32[]{:S(2)}) copy-start(s32[12,2]{0,1:T(2,128)} %param.10) | copy-start | bytes 292
  31.1 33.5 %all-to-all-start.1 = ((bf16[32,2,128,128]{3,2,1,0:T(8,128)(2,1)}), bf16[32,2,128,128]{3,2,1,0:T(8,128)(2,1)}, u32[]{:S(2)}, u32[]{:S(2)}) async-start(bf16[32,2,128,128]{3,2,1,0:T(8,128)(2,1)} %select_select_fusion), calls=%async_computation.1 | async-start | bytes 4194304 | tf_op jit(solution)/shard_map/all_to_all | solution.py:39
  36.1 107.5 %all-gather.2.cloned.1.call-start = ((), (), s32[]{:S(2)}) async-start(), calls=%async_computation.2 | async-start | bytes 7077888 | tf_op jit(solution)/shard_map/all_gather | solution.py:43
  153.4 2.7 copy-start.2
  165.9 2.6 copy-start.3
  170.0 58.3 %collective-permute-start = (bf16[2,256,8,128]{3,1,2,0:T(8,128)(2,1)}, bf16[2,256,8,128]{3,1,2,0:T(8,128)(2,1)S(1)}, u32[]{:S(2)}, u32[]{:S(2)}) collective-permute-start(bf16[2,256,8,128]{3,1,2,0:T(8,128)(2,1)} %pad_maximum_fusion), channel_id=1, source_target_pairs={{0,8},{8,16},{16,24},{24,32},{32,40},{40,48},{48,56},{56,64},{64,7... | collective-permute-start | bytes 3145736 | tf_op jit(solution)/shard_map/ppermute | solution.py:14
  216.2 13.0 %copy-start.5 = (bf16[104,8,8,128]{3,2,1,0:T(8,128)(2,1)S(1)}, bf16[104,8,8,128]{3,2,1,0:T(8,128)(2,1)}, u32[]{:S(2)}) copy-start(bf16[104,8,8,128]{3,2,1,0:T(8,128)(2,1)} %copy.84) | copy-start | bytes 5111812
  233.6 2.8 %copy-start.4 = (f32[13,8,64,256]{3,2,1,0:T(8,128)}, f32[13,8,64,256]{3,2,1,0:T(8,128)S(1)}, u32[]{:S(2)}) copy-start(f32[13,8,64,256]{3,2,1,0:T(8,128)S(1)} %fusion.1) | copy-start | bytes 20447236
  236.4 2.6 copy-start.6
  239.0 21.7 %copy-start.1 = (bf16[1024,1024]{1,0:T(8,128)(2,1)S(1)}, bf16[1024,1024]{1,0:T(8,128)(2,1)}, u32[]{:S(2)}) copy-start(bf16[1024,1024]{1,0:T(8,128)(2,1)} %param.7) | copy-start | bytes 6291460
Sparse Core Ops, SparseCore 0:
  68.0 75.5 all-gather.1
where the time goes:
time: 269 us; the launch traced here: 268 us
  waiting for transfers between devices  104 us (39%)
  local copies, waits for them, and re-layouts  73.5 us (27%)
  matrix products  40.6 us (15%)
  blocking collectives  15.3 us (6%)
  between operations  13.6 us (5%)
  starting transfers between devices  11.6 us (4%)
  other arithmetic  9.01 us (3%)
    all_gather x1, waiting for transfers between devices, on_device(): full_width = lax.all_gather(compact, 'head', axis=2, tiled=True)  75.7 us
    all_to_all x1, waiting for transfers between devices, on_device(): lax.all_to_all(picked, 'seq', split_axis=0, concat_axis=0, tiled=True)  28.2 us
    reshape x2, local copies, waits for them, and re-layouts, on_device(): value_rows.reshape(span_dev, neighbours * block_len, group_heads, HEAD_DIM)  24.1 us
    reshape x2, local copies, waits for them, and re-layouts, on_device(): key_rows.reshape(span_dev, neighbours * block_len, group_heads, HEAD_DIM)  23.9 us
    dot_general x1, matrix products, on_device(): jnp.einsum('chqk,ckhd->cqhd', weights, value_rows, preferred_element_type...  16.8 us
    all_to_all x1, blocking collectives, on_device(): lax.all_to_all(requests, 'seq', split_axis=0, concat_axis=0, tiled=True)  15.3 us
    unnamed x20, local copies, waits for them, and re-layouts  13.1 us
    dot_general x1, matrix products, on_device(): jnp.dot(rows, key_weight, preferred_element_type=jnp.float32)  9.79 us
  transfers between devices with their start and end apart: 3, of which 2 were waited for; matrix products, arithmetic and copies ran while one was open for 19% of the time, Pallas kernels for 0%

commit v1 on v0

--- a/solution.py
+++ b/solution.py
@@ -6,6 +6,19 @@
 
 HEAD_DIM = 128
 SPAN = 64
+
+
+def ring_gather(array, axis, dim):
+    ways = lax.axis_size(axis)
+    up = [(d, (d + 1) % ways) for d in range(ways)]
+    down = [(d, (d - 1) % ways) for d in range(ways)]
+    earlier, later = ([array], [array])
+    for _ in range(ways // 2):
+        earlier.append(lax.ppermute(earlier[-1], axis, up))
+    for _ in range((ways - 1) // 2):
+        later.append(lax.ppermute(later[-1], axis, down))
+    line = jnp.concatenate([*earlier[::-1], *later[1:]], axis=dim)
+    return jnp.roll(line, (lax.axis_index(axis) - ways // 2) * array.shape[dim], axis=dim)
 
 
 def shifted(shard, axis, by):
@@ -40,7 +53,7 @@
     slot_count = replies.shape[1]
     flat_rows = replies.reshape(peer_count * slot_count, block_len, slice_width)
     compact = jnp.take(flat_rows, owner_ids * slot_count + slot_ids, axis=0)
-    full_width = lax.all_gather(compact, "head", axis=2, tiled=True)
+    full_width = ring_gather(compact, "head", 2)
     rows = full_width.reshape(-1, full_width.shape[2])
     key_rows = jnp.dot(rows, key_weight, preferred_element_type=jnp.float32).astype(jnp.bfloat16)
     value_rows = jnp.dot(rows, value_weight, preferred_element_type=jnp.float32).astype(

time: 269 us -> 288 us (1.071)
  local copies, waits for them, and re-layouts: 73.5 us -> 105 us
  between operations: 13.6 us -> 0.26 us
  waiting for transfers between devices: 104 us -> 95.8 us
  starting transfers between devices: 11.6 us -> 19.4 us
    all_gather x1 -> x0, waiting for transfers between devices: 75.7 us -> none  [on_device(): full_width = lax.all_gather(compact, 'head', axis=2, tiled=True)]
    ppermute x0 -> x7, waiting for transfers between devices: none -> 67.6 us  [the longest x4 67.6 us: ring_gather(): earlier.append(lax.ppermute(earlier[-1], axis, up))]
    unnamed x20 -> x43, local copies, waits for them, and re-layouts: 13.1 us -> 39.8 us
    ppermute x0 -> x7, starting transfers between devices: none -> 9.74 us  [the longest x3 8.02 us: ring_gather(): later.append(lax.ppermute(later[-1], axis, down))]
    dynamic_slice x0 -> x1, local copies, waits for them, and re-layouts: none -> 3.49 us  [ring_gather(): jnp.roll(line, (lax.axis_index(axis) - ways // 2) * array.shape[dim], axi...]
  transfers between devices with their start and end apart: 3 -> 9, of which waited for: 2 -> 5; matrix products, arithmetic and copies ran while one was open for 19% -> 23% of each run, Pallas kernels for 0% -> 0%
where the time goes in v1:
time: 288 us; the launch traced here: 284 us
  local copies, waits for them, and re-layouts  105 us (36%)
  waiting for transfers between devices  95.8 us (33%)
  matrix products  38.1 us (13%)
  starting transfers between devices  19.4 us (7%)
  blocking collectives  15.3 us (5%)
  other arithmetic  10.5 us (4%)
    ppermute x4, waiting for transfers between devices, ring_gather(): earlier.append(lax.ppermute(earlier[-1], axis, up))  67.6 us
    unnamed x43, local copies, waits for them, and re-layouts  39.8 us
    all_to_all x1, waiting for transfers between devices, on_device(): lax.all_to_all(picked, 'seq', split_axis=0, concat_axis=0, tiled=True)  28.2 us
    reshape x2, local copies, waits for them, and re-layouts, on_device(): value_rows.reshape(span_dev, neighbours * block_len, group_heads, HEAD_DIM)  24.1 us
    reshape x2, local copies, waits for them, and re-layouts, on_device(): key_rows.reshape(span_dev, neighbours * block_len, group_heads, HEAD_DIM)  24 us
    dot_general x1, matrix products, on_device(): jnp.einsum('chqk,ckhd->cqhd', weights, value_rows, preferred_element_type...  16.8 us
    all_to_all x1, blocking collectives, on_device(): lax.all_to_all(requests, 'seq', split_axis=0, concat_axis=0, tiled=True)  15.3 us
    dot_general x1, matrix products, on_device(): jnp.dot(rows, value_weight, preferred_element_type=jnp.float32)  9.52 us
  transfers between devices with their start and end apart: 9, of which 5 were waited for; matrix products, arithmetic and copies ran while one was open for 23% of the time, Pallas kernels for 0%

profile of v1, /device:TPU:1, one launch (start us, length us, event | category | flops | bytes accessed | tf_op | source)
XLA Modules:
  0.0 284.2 jit_solution(15865549955243313030)
XLA Ops:
  2.3 15.3 %all_to_all.14 = s32[32,1,2]{2,1,0:T(1,128)S(1)} all-to-all(s32[32,1,2]{2,1,0:T(1,128)S(1)} %copy.65), channel_id=1, replica_groups=mesh['seq'=32,'head'=8] {'seq'}, dimensions={0} | all-to-all | bytes 512 | tf_op jit(solution)/shard_map/all_to_all | solution.py:48
  18.2 3.1 %gather_fusion = bf16[64,128,128]{2,1,0:T(8,128)(2,1)} fusion(bf16[8,128,128]{2,1,0:T(8,128)(2,1)} %param.9, s32[1024]{0:T(1024)S(1)} %pad_clamp_fusion.1), kind=kCustom, calls=%fused_computation | custom fusion | bytes 4194560 | tf_op jit(solution)/shard_map/jit(_take)/gather | solution.py:50
  21.3 3.2 %select_select_fusion = bf16[32,2,128,128]{3,2,1,0:T(8,128)(2,1)} fusion(bf16[32,2,128,128]{3,2,1,0:T(8,128)(2,1)} %bitcast.37, pred[32,2]{1,0:T(8,128)(4,1)S(1)} %copy.69, pred[32,2]{1,0:T(8,128)(4,1)S(1)} %copy.67), kind=kLoop, calls=%fused_computation.19 | loop fusion | flops 2097152 | bytes 4194432 | tf_op jit(solution)/shard_map/jit(_where)/select_n | solution.py:51
  24.5 5.0 %all-to-all-start.1 = ((bf16[32,2,128,128]{3,2,1,0:T(8,128)(2,1)}), bf16[32,2,128,128]{3,2,1,0:T(8,128)(2,1)}, u32[]{:S(2)}, u32[]{:S(2)}) async-start(bf16[32,2,128,128]{3,2,1,0:T(8,128)(2,1)} %select_select_fusion), calls=%async_computation.1 | async-start | bytes 4194304 | tf_op jit(solution)/shard_map/all_to_all | solution.py:52
  29.8 28.2 %all-to-all-done.1 = bf16[32,2,128,128]{3,2,1,0:T(8,128)(2,1)} async-done(((bf16[32,2,128,128]{3,2,1,0:T(8,128)(2,1)}), bf16[32,2,128,128]{3,2,1,0:T(8,128)(2,1)}, u32[]{:S(2)}, u32[]{:S(2)}) %all-to-all-start.1) | async-done | bytes 2097184 | tf_op jit(solution)/shard_map/all_to_all | solution.py:52
  62.2 21.0 %collective-permute-done = bf16[24,128,128]{2,1,0:T(8,128)(2,1)S(1)} collective-permute-done((bf16[24,128,128]{2,1,0:T(8,128)(2,1)S(1)}, bf16[24,128,128]{2,1,0:T(8,128)(2,1)S(1)}, u32[]{:S(2)}, u32[]{:S(2)}) %collective-permute-start) | collective-permute-done | bytes 786464 | tf_op jit(solution)/shard_map/ppermute | solution.py:17
  84.1 2.7 collective-permute-start.4
  86.8 16.2 %collective-permute-done.1 = bf16[24,128,128]{2,1,0:T(8,128)(2,1)S(1)} collective-permute-done((bf16[24,128,128]{2,1,0:T(8,128)(2,1)S(1)}, bf16[24,128,128]{2,1,0:T(8,128)(2,1)S(1)}, u32[]{:S(2)}, u32[]{:S(2)}) %collective-permute-start.1) | collective-permute-done | bytes 786464 | tf_op jit(solution)/shard_map/ppermute | solution.py:17
  103.9 2.7 collective-permute-start.5
  106.6 15.5 %collective-permute-done.2 = bf16[24,128,128]{2,1,0:T(8,128)(2,1)} collective-permute-done((bf16[24,128,128]{2,1,0:T(8,128)(2,1)S(1)}, bf16[24,128,128]{2,1,0:T(8,128)(2,1)}, u32[]{:S(2)}, u32[]{:S(2)}) %collective-permute-start.2) | collective-permute-done | bytes 786464 | tf_op jit(solution)/shard_map/ppermute | solution.py:17
  122.1 2.7 collective-permute-start.6
  124.8 14.8 %collective-permute-done.3 = bf16[24,128,128]{2,1,0:T(8,128)(2,1)} collective-permute-done((bf16[24,128,128]{2,1,0:T(8,128)(2,1)}, bf16[24,128,128]{2,1,0:T(8,128)(2,1)}, u32[]{:S(2)}, u32[]{:S(2)}) %collective-permute-start.3) | collective-permute-done | bytes 786464 | tf_op jit(solution)/shard_map/ppermute | solution.py:17
  167.8 3.5 %constant_dynamic-slice_fusion = bf16[24,128,1024]{2,1,0:T(8,128)(2,1)S(1)} fusion(bf16[24,128,2048]{2,1,0:T(8,128)(2,1)} %constant_dynamic-update-slice_fusion, s32[]{:T(128)S(6)} %select_n.55), kind=kLoop, calls=%fused_computation.62 | loop fusion | bytes 12582916 | tf_op jit(solution)/shard_map/jit(_roll_dynamic)/dynamic_slice | solution.py:21
  171.3 7.3 %convolution_convert_fusion.1 = bf16[3072,1024]{0,1:T(8,128)(2,1)S(1)} fusion(bf16[3072,1024]{1,0:T(8,128)(2,1)S(1)} %bitcast.41, bf16[1024,1024]{1,0:T(8,128)(2,1)S(1)} %copy-done), kind=kOutput, calls=%fused_computation.16 | convolution fusion | flops 6445596672 | bytes 14680064 | tf_op jit(solution)/shard_map/dot_general | solution.py:58
  181.7 9.5 %convolution_convert_fusion = bf16[3072,1024]{0,1:T(8,128)(2,1)S(1)} fusion(bf16[3072,1024]{1,0:T(8,128)(2,1)} %bitcast.42, bf16[1024,1024]{1,0:T(8,128)(2,1)} %param.8), kind=kOutput, calls=%fused_computation.15 | convolution fusion | flops 6445596672 | bytes 14680064 | tf_op jit(solution)/shard_map/dot_general | solution.py:59
  195.3 4.6 %collective-permute-start.7 = (bf16[2,256,8,128]{3,1,2,0:T(8,128)(2,1)}, bf16[2,256,8,128]{3,1,2,0:T(8,128)(2,1)S(1)}, u32[]{:S(2)}, u32[]{:S(2)}) collective-permute-start(bf16[2,256,8,128]{3,1,2,0:T(8,128)(2,1)} %pad_maximum_fusion), channel_id=1, source_target_pairs={{0,8},{8,16},{16,24},{24,32},{32,40},{40,48},{48,56},{56,64},{64,7... | collective-permute-start | bytes 3145736 | tf_op jit(solution)/shard_map/ppermute | solution.py:27
  203.5 12.0 %reshape.175 = bf16[12,256,8,128]{1,0,3,2:T(8,128)(2,1)} reshape(bf16[3072,1024]{0,1:T(8,128)(2,1)} %copy-done.2) | data formatting | bytes 12582912 | tf_op jit(solution)/shard_map/reshape | solution.py:63
  215.6 12.1 %reshape.174 = bf16[12,256,8,128]{1,0,3,2:T(8,128)(2,1)} reshape(bf16[3072,1024]{0,1:T(8,128)(2,1)} %copy-done.3) | data formatting | bytes 12582912 | tf_op jit(solution)/shard_map/reshape | solution.py:64
  227.7 11.9 %copy.77 = bf16[12,256,8,128]{3,1,2,0:T(8,128)(2,1)} copy(bf16[12,256,8,128]{1,0,3,2:T(8,128)(2,1)} %reshape.175) | data formatting | bytes 12582912 | tf_op jit(solution)/shard_map/reshape | solution.py:63
  239.6 12.1 %copy.75 = bf16[12,256,8,128]{3,1,2,0:T(8,128)(2,1)} copy(bf16[12,256,8,128]{1,0,3,2:T(8,128)(2,1)} %reshape.174) | data formatting | bytes 12582912 | tf_op jit(solution)/shard_map/reshape | solution.py:64
  252.5 4.5 %fusion.1 = f32[13,8,64,256]{3,2,1,0:T(8,128)S(1)} fusion(bf16[12,256,8,128]{3,1,2,0:T(8,128)(2,1)} %copy.77, bf16[1,256,8,128]{3,1,2,0:T(8,128)(2,1)S(1)} %get-tuple-element.5, bf16[13,64,8,128]{3,2,1,0:T(8,128)(2,1)S(1)} %bitcast.39), kind=kOutput, calls=%fused_computation.3 | convolution fusion | flops 439615488 | bytes 15335424 | tf_op jit(solution)/shard_map/cqhd,ckhd->chqk/dot_general | solution.py:74
  257.1 2.8 copy-done.4
  262.5 16.8 %fusion.18 = bf16[13,64,8,128]{3,1,2,0:T(8,128)(2,1)} fusion(bf16[12,256,8,128]{3,1,2,0:T(8,128)(2,1)} %copy.75, bf16[1,256,8,128]{3,1,2,0:T(8,128)(2,1)S(1)} %copy-done.11, f32[13,8,64]{2,1,0:T(8,128)S(1)} %fusion.34, f32[13,8,64,256]{3,2,1,0:T(8,128)} %copy-done.4), kind=kOutput, calls=%fused_computation.24 | convolution fusion | flops 459217664 | bytes 15362048 | tf_op jit(solution)/shard_map/chqk,ckhd->cqhd/dot_general | solution.py:78
  279.3 2.8 copy.79
  (86 shorter events, 53.4 us)
Async XLA Ops:
  0.0 171.3 %copy-start = (bf16[1024,1024]{1,0:T(8,128)(2,1)S(1)}, bf16[1024,1024]{1,0:T(8,128)(2,1)}, u32[]{:S(2)}) copy-start(bf16[1024,1024]{1,0:T(8,128)(2,1)} %param.7) | copy-start | bytes 6291460
  0.0 29.6 %copy-start.12 = (s32[12,2]{0,1:T(2,128)S(1)}, s32[12,2]{0,1:T(2,128)}, u32[]{:S(2)}) copy-start(s32[12,2]{0,1:T(2,128)} %param.10) | copy-start | bytes 292
  24.5 33.5 %all-to-all-start.1 = ((bf16[32,2,128,128]{3,2,1,0:T(8,128)(2,1)}), bf16[32,2,128,128]{3,2,1,0:T(8,128)(2,1)}, u32[]{:S(2)}, u32[]{:S(2)}) async-start(bf16[32,2,128,128]{3,2,1,0:T(8,128)(2,1)} %select_select_fusion), calls=%async_computation.1 | async-start | bytes 4194304 | tf_op jit(solution)/shard_map/all_to_all | solution.py:52
  60.5 22.8 %collective-permute-start = (bf16[24,128,128]{2,1,0:T(8,128)(2,1)S(1)}, bf16[24,128,128]{2,1,0:T(8,128)(2,1)S(1)}, u32[]{:S(2)}, u32[]{:S(2)}) collective-permute-start(bf16[24,128,128]{2,1,0:T(8,128)(2,1)S(1)} %broadcast_select_fusion), channel_id=1, source_target_pairs={{0,1},{1,2},{2,3},{3,4},{4,5},{5,6},{6,7},{7,0},{8,9},{9,10},{10,1... | collective-permute-start | bytes 2359304 | tf_op jit(solution)/shard_map/ppermute | solution.py:17
  83.2 0.9 copy-start.7
  84.1 18.9 %collective-permute-start.1 = (bf16[24,128,128]{2,1,0:T(8,128)(2,1)S(1)}, bf16[24,128,128]{2,1,0:T(8,128)(2,1)S(1)}, u32[]{:S(2)}, u32[]{:S(2)}) collective-permute-start(bf16[24,128,128]{2,1,0:T(8,128)(2,1)S(1)} %collective-permute-done), channel_id=1, source_target_pairs={{0,1},{1,2},{2,3},{3,4},{4,5},{5,6},{6,7},{7,0},{8,9},{9,10},{10,1... | collective-permute-start | bytes 2359304 | tf_op jit(solution)/shard_map/ppermute | solution.py:17
  84.1 19.8 %collective-permute-start.4 = (bf16[24,128,128]{2,1,0:T(8,128)(2,1)S(1)}, bf16[24,128,128]{2,1,0:T(8,128)(2,1)}, u32[]{:S(2)}, u32[]{:S(2)}) collective-permute-start(bf16[24,128,128]{2,1,0:T(8,128)(2,1)S(1)} %broadcast_select_fusion), channel_id=1, source_target_pairs={{0,7},{1,0},{2,1},{3,2},{4,3},{5,4},{6,5},{7,6},{8,15},{9,8},{10,9... | collective-permute-start | bytes 2359304 | tf_op jit(solution)/shard_map/ppermute | solution.py:19
  103.0 0.9 copy-start.9
  103.9 18.2 %collective-permute-start.2 = (bf16[24,128,128]{2,1,0:T(8,128)(2,1)S(1)}, bf16[24,128,128]{2,1,0:T(8,128)(2,1)}, u32[]{:S(2)}, u32[]{:S(2)}) collective-permute-start(bf16[24,128,128]{2,1,0:T(8,128)(2,1)S(1)} %collective-permute-done.1), channel_id=1, source_target_pairs={{0,1},{1,2},{2,3},{3,4},{4,5},{5,6},{6,7},{7,0},{8,9},{9,10},{10,1... | collective-permute-start | bytes 2359304 | tf_op jit(solution)/shard_map/ppermute | solution.py:17
  103.9 18.2 %collective-permute-start.5 = (bf16[24,128,128]{2,1,0:T(8,128)(2,1)}, bf16[24,128,128]{2,1,0:T(8,128)(2,1)}, u32[]{:S(2)}, u32[]{:S(2)}) collective-permute-start(bf16[24,128,128]{2,1,0:T(8,128)(2,1)} %collective-permute-done.4), channel_id=1, source_target_pairs={{0,7},{1,0},{2,1},{3,2},{4,3},{5,4},{6,5},{7,6},{8,15},{9,8},{10,9... | collective-permute-start | bytes 2359304 | tf_op jit(solution)/shard_map/ppermute | solution.py:19
  122.1 17.5 %collective-permute-start.3 = (bf16[24,128,128]{2,1,0:T(8,128)(2,1)}, bf16[24,128,128]{2,1,0:T(8,128)(2,1)}, u32[]{:S(2)}, u32[]{:S(2)}) collective-permute-start(bf16[24,128,128]{2,1,0:T(8,128)(2,1)} %collective-permute-done.2), channel_id=1, source_target_pairs={{0,1},{1,2},{2,3},{3,4},{4,5},{5,6},{6,7},{7,0},{8,9},{9,10},{10,1... | collective-permute-start | bytes 2359304 | tf_op jit(solution)/shard_map/ppermute | solution.py:17
  122.1 31.8 %collective-permute-start.6 = (bf16[24,128,128]{2,1,0:T(8,128)(2,1)}, bf16[24,128,128]{2,1,0:T(8,128)(2,1)S(1)}, u32[]{:S(2)}, u32[]{:S(2)}) collective-permute-start(bf16[24,128,128]{2,1,0:T(8,128)(2,1)} %collective-permute-done.5), channel_id=1, source_target_pairs={{0,7},{1,0},{2,1},{3,2},{4,3},{5,4},{6,5},{7,6},{8,15},{9,8},{10,9... | collective-permute-start | bytes 2359304 | tf_op jit(solution)/shard_map/ppermute | solution.py:19
  141.7 17.6 %copy-start.10 = (bf16[24,128,128]{2,1,0:T(8,128)(2,1)S(1)}, bf16[24,128,128]{2,1,0:T(8,128)(2,1)}, u32[]{:S(2)}) copy-start(bf16[24,128,128]{2,1,0:T(8,128)(2,1)} %copy-done.9) | copy-start | bytes 2359300
  144.0 16.4 %copy-start.8 = (bf16[24,128,128]{2,1,0:T(8,128)(2,1)S(1)}, bf16[24,128,128]{2,1,0:T(8,128)(2,1)}, u32[]{:S(2)}) copy-start(bf16[24,128,128]{2,1,0:T(8,128)(2,1)} %copy-done.7) | copy-start | bytes 2359300
  171.3 7.3 %copy-start.6 = (bf16[24,128,1024]{2,1,0:T(8,128)(2,1)}, bf16[24,128,1024]{2,1,0:T(8,128)(2,1)S(1)}, u32[]{:S(2)}) copy-start(bf16[24,128,1024]{2,1,0:T(8,128)(2,1)S(1)} %constant_dynamic-slice_fusion) | copy-start | bytes 18874372
  178.7 2.7 copy-start.2
  191.2 2.7 copy-start.3
  195.3 56.4 %collective-permute-start.7 = (bf16[2,256,8,128]{3,1,2,0:T(8,128)(2,1)}, bf16[2,256,8,128]{3,1,2,0:T(8,128)(2,1)S(1)}, u32[]{:S(2)}, u32[]{:S(2)}) collective-permute-start(bf16[2,256,8,128]{3,1,2,0:T(8,128)(2,1)} %pad_maximum_fusion), channel_id=1, source_target_pairs={{0,8},{8,16},{16,24},{24,32},{32,40},{40,48},{48,56},{56,64},{64,7... | collective-permute-start | bytes 3145736 | tf_op jit(solution)/shard_map/ppermute | solution.py:27
  239.6 12.9 %copy-start.5 = (bf16[104,8,8,128]{3,2,1,0:T(8,128)(2,1)S(1)}, bf16[104,8,8,128]{3,2,1,0:T(8,128)(2,1)}, u32[]{:S(2)}) copy-start(bf16[104,8,8,128]{3,2,1,0:T(8,128)(2,1)} %copy.84) | copy-start | bytes 5111812
  257.0 2.8 copy-start.4
  259.9 2.6 copy-start.11
  262.5 21.7 %copy-start.1 = (bf16[1024,1024]{1,0:T(8,128)(2,1)S(1)}, bf16[1024,1024]{1,0:T(8,128)(2,1)}, u32[]{:S(2)}) copy-start(bf16[1024,1024]{1,0:T(8,128)(2,1)} %param.7) | copy-start | bytes 6291460
